TPU v7x, 32 devices: a whole 2x2x4 slice. The times are simulated.
32 devices in a mesh: groups: 2 (over x), rows: 16 (over z, y, core).
Axes of the slice: x: 2, y: 2, z: 4, core: 2. Of those that a mesh axis runs over, the one named last changes fastest.
Arguments:
- tokens: bfloat16 [64, 256, 1024], P(('groups', 'rows')), parts along dimension 0, may hold values from -6 to 6
- peg_weight: float32 [3, 3, 1024], replicated, may hold values from -2 to 2
- peg_bias: float32 [1024], replicated, may hold values from -3 to 3
- norm_gain: float32 [1024], replicated, may hold values from 0.25 to 1.75
- norm_bias: float32 [1024], replicated, may hold values from -3 to 3
- qkv_weight: bfloat16 [1024, 3072], replicated, may hold values from -1 to 1
- qkv_bias: float32 [3072], replicated, may hold values from -3 to 3
- out_weight: bfloat16 [1024, 1024], replicated, may hold values from -0.1875 to 0.1875
- out_bias: float32 [1024], replicated, may hold values from -3 to 3
Outputs:
- result: bfloat16 [64, 256, 1024], P(('groups', 'rows')), parts along dimension 0
There are 2 independent parts, one for each index of `groups`. A program takes and returns all parts, laid end to end along the dimension named above; an argument that names none is the same for every part. Nothing has to cross between parts.
All inputs are finite; a program needn't handle non-finite values.
Results may differ from a plain program's by a relative error of at most 0.006.
Values may be sent and summed in bfloat16 or wider, within the bound.
No kernel may reach another device: no remote copies, remote signals or barrier semaphores. Data moves between devices by JAX's collectives and lax.ppermute only.
A program may use at most 64 MiB of HBM per device.

v0:
```python
import math
import jax
import jax.numpy as jnp
from jax import lax
from jax.sharding import PartitionSpec as P

HEADS = 16
DH = 64
ROW_HEADS = 8


def with_halo(value, sides, width):
    for axis, dim in sides:
        devices, length = (lax.axis_size(axis), value.shape[dim])
        up = [(i, (i + 1) % devices) for i in range(devices - 1)]
        down = [(j, i) for i, j in up]
        last = lax.slice_in_dim(value, length - width, length, axis=dim)
        leading = lax.slice_in_dim(value, 0, width, axis=dim)
        before = lax.ppermute(last, axis, up)
        after = lax.ppermute(leading, axis, down)
        value = jnp.concatenate([before, value, after], axis=dim)
    return value


def convolve(padded, peg_weight, peg_bias, count_rows, count_cols):
    total = padded[1 : count_rows + 1, 1 : count_cols + 1, :].astype(jnp.float32) + peg_bias
    for offset_row in range(3):
        for offset_col in range(3):
            piece = padded[
                offset_row : offset_row + count_rows, offset_col : offset_col + count_cols, :
            ]
            total = total + piece.astype(jnp.float32) * peg_weight[offset_row, offset_col]
    return total.astype(jnp.bfloat16)


def layer_norm(mixed, norm_gain, norm_bias):
    values = mixed.astype(jnp.float32)
    center = jnp.mean(values, axis=-1, keepdims=True)
    spread = jnp.mean((values - center) ** 2, axis=-1, keepdims=True)
    return ((values - center) * lax.rsqrt(spread + 1e-06) * norm_gain + norm_bias).astype(
        jnp.bfloat16
    )


def project_three(normed, qkv_weight, qkv_bias, first_col, last_col):
    model = normed.shape[-1]
    flat_rows = normed.reshape(-1, model)
    outputs = []
    for part_index in range(3):
        lower = part_index * model + first_col
        upper = part_index * model + last_col
        projected = (
            jnp.dot(flat_rows, qkv_weight[:, lower:upper], preferred_element_type=jnp.float32)
            + qkv_bias[lower:upper]
        )
        outputs.append(
            projected.astype(jnp.bfloat16).reshape(normed.shape[:-1] + (last_col - first_col,))
        )
    return (outputs[0], outputs[1], outputs[2])


def attend_heads(
    query_all, key_all, value_all, head_count, softmax_divisor, scoring_equation, mixing_equation
):
    outputs = []
    for head_index in range(head_count):
        lower = head_index * DH
        query_rows = query_all[..., lower : lower + DH]
        key_operand = key_all[..., lower : lower + DH]
        value_operand = value_all[..., lower : lower + DH]
        attention_logits = (
            jnp.einsum(
                scoring_equation, query_rows, key_operand, preferred_element_type=jnp.float32
            )
            * softmax_divisor
        )
        highest = jnp.max(attention_logits, axis=-1, keepdims=True)
        attention_weights = jnp.exp(attention_logits - highest)
        attention_weights = (
            attention_weights / jnp.sum(attention_weights, axis=-1, keepdims=True)
        ).astype(jnp.bfloat16)
        outputs.append(
            jnp.einsum(
                mixing_equation,
                attention_weights,
                value_operand,
                preferred_element_type=jnp.float32,
            ).astype(jnp.bfloat16)
        )
    return jnp.concatenate(outputs, axis=-1)


def on_device(
    tokens, peg_weight, peg_bias, norm_gain, norm_bias, qkv_weight, qkv_bias, out_weight, out_bias
):
    bands = tokens.shape[0]
    width = tokens.shape[1]
    model = tokens.shape[2]
    height = bands * lax.axis_size("rows")
    row_features = ROW_HEADS * DH
    col_count = HEADS - ROW_HEADS
    padded = with_halo(tokens, (("rows", 0),), 1)
    padded = jnp.pad(padded, ((0, 0), (1, 1), (0, 0)))
    mixed = convolve(padded, peg_weight, peg_bias, bands, width)
    normed = layer_norm(mixed, norm_gain, norm_bias)
    row_query, row_key, row_value = project_three(normed, qkv_weight, qkv_bias, 0, row_features)
    arrived = lax.all_to_all(normed, "rows", split_axis=1, concat_axis=0, tiled=True)
    col_query, col_key, col_value = project_three(
        arrived, qkv_weight, qkv_bias, row_features, model
    )
    tau_row = math.log(width) / (math.log(16.0) * math.sqrt(DH))
    tau_col = math.log(height) / (math.log(16.0) * math.sqrt(DH))
    row_heads = attend_heads(
        row_query, row_key, row_value, ROW_HEADS, tau_row, "bld,bmd->blm", "blm,bmd->bld"
    )
    col_heads = attend_heads(
        col_query, col_key, col_value, col_count, tau_col, "lbd,mbd->blm", "blm,mbd->lbd"
    )
    returned = lax.all_to_all(col_heads, "rows", split_axis=0, concat_axis=1, tiled=True)
    attended = jnp.concatenate([row_heads, returned], axis=2).reshape(bands * width, model)
    result = (
        mixed.reshape(bands * width, model).astype(jnp.float32)
        + jnp.dot(attended, out_weight, preferred_element_type=jnp.float32)
        + out_bias
    )
    return result.astype(jnp.bfloat16).reshape(bands, width, model)


def solution(mesh):
    placed = (P(("groups", "rows"), None, None), P(), P(), P(), P(), P(), P(), P(), P())
    return jax.shard_map(
        on_device,
        mesh=mesh,
        in_specs=placed,
        out_specs=P(("groups", "rows"), None, None),
        check_vma=False,
    )
```

profile of v0, /device:TPU:0, one launch (start us, length us, event | category | flops | bytes accessed | tf_op | source)
XLA Modules:
  0.0 165.9 jit_solution(17638637918727739005)
XLA Ops:
  1.4 2.4 %collective-permute-start = (bf16[1,256,1024]{2,1,0:T(8,128)(2,1)S(1)}, bf16[1,256,1024]{2,1,0:T(8,128)(2,1)S(1)}, u32[]{:S(2)}, u32[]{:S(2)}) collective-permute-start(bf16[1,256,1024]{2,1,0:T(8,128)(2,1)S(1)} %get-tuple-element.7), channel_id=1, source_target_pairs={{0,1},{1,2},{2,3},{3,4},{4,5},{5,6},{6,7},{7,8},{8,9},{9,10},{10,1... | collective-permute-start | bytes 1572872 | tf_op jit(solution)/shard_map/ppermute | solution.py:19
  5.3 4.4 %collective-permute-done.1 = bf16[1,256,1024]{2,1,0:T(8,128)(2,1)S(1)} collective-permute-done((bf16[1,256,1024]{2,1,0:T(8,128)(2,1)S(1)}, bf16[1,256,1024]{2,1,0:T(8,128)(2,1)S(1)}, u32[]{:S(2)}, u32[]{:S(2)}) %collective-permute-start.1) | collective-permute-done | bytes 524320 | tf_op jit(solution)/shard_map/ppermute | solution.py:20
  10.5 2.6 %convert_reduce_fusion = (f32[2,256]{1,0:T(2,128)S(1)}, bf16[2,256,1024]{2,1,0:T(8,128)(2,1)S(1)}) fusion(f32[1024]{0:T(1024)S(1)} %bitcast.137, bf16[4,258,1024]{2,1,0:T(8,128)(2,1)S(1)} %fusion.21, f32[1024]{0:T(1024)S(1)} %bitcast.138, bf16[1,256,1024]{2,1,0:T(8,128)(2,1)S(1)} %collective-permute-done.1, bf16[2,256,1024]{2,1,0:T(8,128)(2,1)S(1)} %copy-done.1, ...), kind=kLoop, calls=%fused_computation.41 | loop fusion | flops 17300992 | bytes 9480192 | tf_op jit(solution)/shard_map/reduce_sum | solution.py:38
  14.0 3.1 %fusion.35 = bf16[512,512]{1,0:T(8,128)(2,1)} fusion(bf16[512,1024]{1,0:T(8,128)(2,1)S(1)} %bitcast.79, bf16[1024,3072]{1,0:T(8,128)(2,1)} %param.14, f32[512]{0:T(512)S(1)} %get-tuple-element.45), kind=kOutput, calls=%fused_computation.49 | convolution fusion | flops 537395200 | bytes 2623488 | tf_op jit(solution)/shard_map/dot_general | solution.py:53
  17.1 2.8 %fusion.34 = bf16[512,512]{1,0:T(8,128)(2,1)} fusion(bf16[512,1024]{1,0:T(8,128)(2,1)S(1)} %bitcast.80, bf16[1024,3072]{1,0:T(8,128)(2,1)} %param.14, f32[512]{0:T(512)S(1)} %get-tuple-element.46), kind=kOutput, calls=%fused_computation.48 | convolution fusion | flops 537395200 | bytes 2623488 | tf_op jit(solution)/shard_map/dot_general | solution.py:53
  28.7 2.1 %convolution_multiply_fusion.2 = f32[2,256,256]{1,2,0:T(8,128)} fusion(bf16[2,256,512]{2,1,0:T(8,128)(2,1)} %bitcast.91, bf16[2,256,512]{2,1,0:T(8,128)(2,1)} %bitcast.107), kind=kOutput, calls=%fused_computation.72 | convolution fusion | flops 16908288 | bytes 786432 | tf_op jit(solution)/shard_map/bld,bmd->blm/dot_general | solution.py:72
  32.9 2.7 %fusion.36 = bf16[512,512]{1,0:T(8,128)(2,1)} fusion(bf16[512,1024]{1,0:T(8,128)(2,1)S(1)} %bitcast.81, bf16[1024,3072]{1,0:T(8,128)(2,1)} %param.14, f32[512]{0:T(512)S(1)} %get-tuple-element.44), kind=kOutput, calls=%fused_computation.50 | convolution fusion | flops 537395200 | bytes 2623488 | tf_op jit(solution)/shard_map/dot_general | solution.py:53
  35.6 14.6 %all-to-all-start = ((bf16[2,256,1024]{2,0,1:T(2,128)(2,1)}), bf16[2,256,1024]{2,0,1:T(2,128)(2,1)}, u32[]{:S(2)}, u32[]{:S(2)}) async-start(bf16[2,256,1024]{2,0,1:T(2,128)(2,1)} %copy.367), calls=%async_computation | async-start | bytes 2097152 | tf_op jit(solution)/shard_map/all_to_all | solution.py:107
  50.3 2.1 %convolution_convert_fusion.9 = bf16[2,256,64]{1,2,0:T(8,128)(2,1)} fusion(f32[2,256]{1,0:T(2,128)S(1)} %fusion.275, bf16[2,256,512]{2,1,0:T(8,128)(2,1)} %bitcast.139, f32[2,256,256]{1,2,0:T(8,128)} %convolution_multiply_fusion.1), kind=kOutput, calls=%fused_computation.119 | convolution fusion | flops 17203968 | bytes 1247232 | tf_op jit(solution)/shard_map/blm,bmd->bld/dot_general | solution.py:83
  52.4 2.2 %convolution_convert_fusion.10 = bf16[2,256,64]{1,2,0:T(8,128)(2,1)} fusion(f32[2,256]{1,0:T(2,128)S(1)} %fusion.270, bf16[2,256,512]{2,1,0:T(8,128)(2,1)} %bitcast.140, f32[2,256,256]{1,2,0:T(8,128)} %convolution_multiply_fusion.2), kind=kOutput, calls=%fused_computation.120 | convolution fusion | flops 17203968 | bytes 1247232 | tf_op jit(solution)/shard_map/blm,bmd->bld/dot_general | solution.py:83
  58.6 2.2 %convolution_convert_fusion.11 = bf16[2,256,64]{1,2,0:T(8,128)(2,1)} fusion(f32[2,256]{1,0:T(2,128)S(1)} %fusion.265, bf16[2,256,512]{2,1,0:T(8,128)(2,1)} %bitcast.141, f32[2,256,256]{1,2,0:T(8,128)} %convolution_multiply_fusion.3), kind=kOutput, calls=%fused_computation.121 | convolution fusion | flops 17203968 | bytes 1247232 | tf_op jit(solution)/shard_map/blm,bmd->bld/dot_general | solution.py:83
  60.7 2.1 %convolution_multiply_fusion.4 = f32[2,256,256]{1,2,0:T(8,128)} fusion(bf16[2,256,512]{2,1,0:T(8,128)(2,1)} %bitcast.94, bf16[2,256,512]{2,1,0:T(8,128)(2,1)} %bitcast.110), kind=kOutput, calls=%fused_computation.74 | convolution fusion | flops 16908288 | bytes 786432 | tf_op jit(solution)/shard_map/bld,bmd->blm/dot_general | solution.py:72
  62.8 2.2 %convolution_convert_fusion.12 = bf16[2,256,64]{1,2,0:T(8,128)(2,1)} fusion(f32[2,256]{1,0:T(2,128)S(1)} %fusion.260, bf16[2,256,512]{2,1,0:T(8,128)(2,1)} %bitcast.142, f32[2,256,256]{1,2,0:T(8,128)} %convolution_multiply_fusion.4), kind=kOutput, calls=%fused_computation.122 | convolution fusion | flops 17203968 | bytes 1247232 | tf_op jit(solution)/shard_map/blm,bmd->bld/dot_general | solution.py:83
  67.0 2.2 %convolution_convert_fusion.13 = bf16[2,256,64]{1,2,0:T(8,128)(2,1)} fusion(f32[2,256]{1,0:T(2,128)S(1)} %fusion.255, bf16[2,256,512]{2,1,0:T(8,128)(2,1)} %bitcast.143, f32[2,256,256]{1,2,0:T(8,128)} %convolution_multiply_fusion.5), kind=kOutput, calls=%fused_computation.123 | convolution fusion | flops 17203968 | bytes 1247232 | tf_op jit(solution)/shard_map/blm,bmd->bld/dot_general | solution.py:83
  74.9 2.3 %fusion.39 = bf16[512,512]{1,0:T(8,128)(2,1)S(1)} fusion(bf16[512,1024]{1,0:T(8,128)(2,1)S(1)} %bitcast.119, bf16[1024,3072]{1,0:T(8,128)(2,1)} %param.14, f32[512]{0:T(512)S(1)} %get-tuple-element.47), kind=kOutput, calls=%fused_computation.53 | convolution fusion | flops 537395200 | bytes 2623488 | tf_op jit(solution)/shard_map/dot_general | solution.py:53
  107.3 2.2 %fusion.37 = bf16[512,512]{1,0:T(8,128)(2,1)S(1)} fusion(bf16[512,1024]{1,0:T(8,128)(2,1)} %bitcast.121, bf16[1024,3072]{1,0:T(8,128)(2,1)} %param.14, f32[512]{0:T(512)S(1)} %get-tuple-element.43), kind=kOutput, calls=%fused_computation.51 | convolution fusion | flops 537395200 | bytes 2623488 | tf_op jit(solution)/shard_map/dot_general | solution.py:53
  125.3 2.1 %concatenate.45 = bf16[32,16,512]{2,0,1:T(8,128)(2,1)} concatenate(bf16[32,16,64]{2,0,1:T(8,128)(2,1)S(1)} %fusion.72, bf16[32,16,64]{2,0,1:T(8,128)(2,1)} %fusion.73, bf16[32,16,64]{2,0,1:T(8,128)(2,1)} %fusion.74, bf16[32,16,64]{2,0,1:T(8,128)(2,1)} %fusion.75, bf16[32,16,64]{2,0,1:T(8,128)(2,1)} %fusion.76, bf16[32,16,64]{2,0,1:T(8,128)(2,1)} %fusion.77, ...), dimensions={2} | concatenate | bytes 1048576 | tf_op jit(solution)/shard_map/concatenate | solution.py:90
  127.4 2.2 %copy.402 = bf16[32,16,512]{2,1,0:T(8,128)(2,1)} copy(bf16[32,16,512]{2,0,1:T(8,128)(2,1)} %concatenate.45) | data formatting | bytes 1048576 | tf_op jit(solution)/shard_map/concatenate | solution.py:90
  129.6 6.9 %all-to-all-start.1 = ((bf16[32,16,512]{2,1,0:T(8,128)(2,1)}), bf16[32,16,512]{2,1,0:T(8,128)(2,1)}, u32[]{:S(2)}, u32[]{:S(2)}) async-start(bf16[32,16,512]{2,1,0:T(8,128)(2,1)} %copy.402), calls=%async_computation.1 | async-start | bytes 1048576 | tf_op jit(solution)/shard_map/all_to_all | solution.py:119
  136.6 2.2 %convolution_convert_fusion.14 = bf16[2,256,64]{1,2,0:T(8,128)(2,1)} fusion(f32[2,256]{1,0:T(2,128)S(1)} %copy-done.16, bf16[2,256,512]{2,1,0:T(8,128)(2,1)} %bitcast.144, f32[2,256,256]{1,2,0:T(8,128)} %convolution_multiply_fusion.6), kind=kOutput, calls=%fused_computation.124 | convolution fusion | flops 17203968 | bytes 1247232 | tf_op jit(solution)/shard_map/blm,bmd->bld/dot_general | solution.py:83
  146.1 2.2 %convolution_convert_fusion.15 = bf16[2,256,64]{1,2,0:T(8,128)(2,1)} fusion(f32[2,256]{1,0:T(2,128)S(1)} %fusion.245, bf16[2,256,512]{2,1,0:T(8,128)(2,1)} %bitcast.145, f32[2,256,256]{1,2,0:T(8,128)} %convolution_multiply_fusion.7), kind=kOutput, calls=%fused_computation.125 | convolution fusion | flops 17203968 | bytes 1247232 | tf_op jit(solution)/shard_map/blm,bmd->bld/dot_general | solution.py:83
  153.3 2.1 %convolution_convert_fusion.8 = bf16[2,256,64]{1,2,0:T(8,128)(2,1)} fusion(f32[2,256]{1,0:T(2,128)S(1)} %fusion.280, bf16[2,256,512]{2,1,0:T(8,128)(2,1)} %bitcast.146, f32[2,256,256]{1,2,0:T(8,128)} %convolution_multiply_fusion), kind=kOutput, calls=%fused_computation.118 | convolution fusion | flops 17203968 | bytes 1247232 | tf_op jit(solution)/shard_map/blm,bmd->bld/dot_general | solution.py:83
  158.9 3.5 %concatenate.47 = bf16[512,1024]{1,0:T(8,128)(2,1)} concatenate(bf16[512,64]{1,0:T(8,128)(2,1)} %bitcast.128, bf16[512,64]{1,0:T(8,128)(2,1)} %bitcast.127, bf16[512,64]{1,0:T(8,128)(2,1)} %bitcast.126, bf16[512,64]{1,0:T(8,128)(2,1)} %bitcast.125, bf16[512,64]{1,0:T(8,128)(2,1)S(1)} %bitcast.124, bf16[512,64]{1,0:T(8,128)(2,1)S(1)} %bitcast.123, bf16[512,64]{1,0:T(8,128)(2,1)S(1)} %bitcast.122, ...), dimensions={1} | concatenate | bytes 2097152 | tf_op jit(solution)/shard_map/concatenate | solution.py:120
  162.4 3.5 %fusion.33 = bf16[512,1024]{1,0:T(8,128)(2,1)} fusion(bf16[2,256,1024]{2,1,0:T(8,128)(2,1)S(1)} %get-tuple-element.6, bf16[512,1024]{1,0:T(8,128)(2,1)} %concatenate.47, bf16[1024,1024]{1,0:T(8,128)(2,1)S(1)} %copy-done, f32[1024]{0:T(1024)S(1)} %copy-done.12), kind=kOutput, calls=%fused_computation.38 | convolution fusion | flops 1075838976 | bytes 5246976 | tf_op jit(solution)/shard_map/dot_general | solution.py:123
  (99 shorter events, 88.7 us)
Async XLA Ops:
  0.0 162.4 %copy-start = (bf16[1024,1024]{1,0:T(8,128)(2,1)S(1)}, bf16[1024,1024]{1,0:T(8,128)(2,1)}, u32[]{:S(2)}) copy-start(bf16[1024,1024]{1,0:T(8,128)(2,1)} %param.16) | copy-start | bytes 6291460
  0.0 9.7 %copy-start.1 = (bf16[2,256,1024]{2,1,0:T(8,128)(2,1)S(1)}, bf16[2,256,1024]{2,1,0:T(8,128)(2,1)}, u32[]{:S(2)}) copy-start(bf16[2,256,1024]{2,1,0:T(8,128)(2,1)} %param.9) | copy-start | bytes 3145732
  0.0 5.1 %copy-start.8 = (f32[3072]{0:T(1024)S(1)}, f32[3072]{0:T(1024)}, u32[]{:S(2)}) copy-start(f32[3072]{0:T(1024)} %param.15) | copy-start | bytes 36868
  0.0 5.2 %copy-start.7 = (f32[3,3,1024]{2,1,0:T(4,128)S(1)}, f32[3,3,1024]{2,1,0:T(4,128)}, u32[]{:S(2)}) copy-start(f32[3,3,1024]{2,1,0:T(4,128)} %param.10) | copy-start | bytes 110596
  1.4 3.9 %collective-permute-start = (bf16[1,256,1024]{2,1,0:T(8,128)(2,1)S(1)}, bf16[1,256,1024]{2,1,0:T(8,128)(2,1)S(1)}, u32[]{:S(2)}, u32[]{:S(2)}) collective-permute-start(bf16[1,256,1024]{2,1,0:T(8,128)(2,1)S(1)} %get-tuple-element.7), channel_id=1, source_target_pairs={{0,1},{1,2},{2,3},{3,4},{4,5},{5,6},{6,7},{7,8},{8,9},{9,10},{10,1... | collective-permute-start | bytes 1572872 | tf_op jit(solution)/shard_map/ppermute | solution.py:19
  3.8 5.9 %collective-permute-start.1 = (bf16[1,256,1024]{2,1,0:T(8,128)(2,1)S(1)}, bf16[1,256,1024]{2,1,0:T(8,128)(2,1)S(1)}, u32[]{:S(2)}, u32[]{:S(2)}) collective-permute-start(bf16[1,256,1024]{2,1,0:T(8,128)(2,1)S(1)} %get-tuple-element.8), channel_id=1, source_target_pairs={{1,0},{2,1},{3,2},{4,3},{5,4},{6,5},{7,6},{8,7},{9,8},{10,9},{11,1... | collective-permute-start | bytes 1572872 | tf_op jit(solution)/shard_map/ppermute | solution.py:20
  5.2 5.2 %copy-start.9 = (f32[1024]{0:T(1024)S(1)}, f32[1024]{0:T(1024)}, u32[]{:S(2)}) copy-start(f32[1024]{0:T(1024)} %param.11) | copy-start | bytes 12292
  10.4 3.1 %copy-start.10 = (f32[1024]{0:T(1024)S(1)}, f32[1024]{0:T(1024)}, u32[]{:S(2)}) copy-start(f32[1024]{0:T(1024)} %param.13) | copy-start | bytes 12292
  10.4 3.1 %copy-start.11 = (f32[1024]{0:T(1024)S(1)}, f32[1024]{0:T(1024)}, u32[]{:S(2)}) copy-start(f32[1024]{0:T(1024)} %param.12) | copy-start | bytes 12292
  14.0 5.9 %copy-start.2 = (bf16[2,256,1024]{2,1,0:T(8,128)(2,1)}, bf16[2,256,1024]{2,1,0:T(8,128)(2,1)S(1)}, u32[]{:S(2)}) copy-start(bf16[2,256,1024]{2,1,0:T(8,128)(2,1)S(1)} %add_convert_fusion) | copy-start | bytes 3145732
  26.7 4.2 %copy-start.3 = (bf16[2,256,1024]{2,1,0:T(8,128)(2,1)S(1)}, bf16[2,256,1024]{2,1,0:T(8,128)(2,1)}, u32[]{:S(2)}) copy-start(bf16[2,256,1024]{2,1,0:T(8,128)(2,1)} %copy-done.2) | copy-start | bytes 3145732
  35.6 37.6 %all-to-all-start = ((bf16[2,256,1024]{2,0,1:T(2,128)(2,1)}), bf16[2,256,1024]{2,0,1:T(2,128)(2,1)}, u32[]{:S(2)}, u32[]{:S(2)}) async-start(bf16[2,256,1024]{2,0,1:T(2,128)(2,1)} %copy.367), calls=%async_computation | async-start | bytes 2097152 | tf_op jit(solution)/shard_map/all_to_all | solution.py:107
  74.9 4.3 %copy-start.4 = (bf16[16,2,16,1024]{3,2,1,0:T(8,128)(2,1)}, bf16[16,2,16,1024]{3,2,1,0:T(8,128)(2,1)S(1)}, u32[]{:S(2)}) copy-start(bf16[16,2,16,1024]{3,2,1,0:T(8,128)(2,1)S(1)} %copy.369) | copy-start | bytes 3145732
  111.9 6.1 %copy-start.13 = (f32[16,32]{1,0:T(8,128)S(1)}, f32[16,32]{1,0:T(8,128)}, u32[]{:S(2)}) copy-start(f32[16,32]{1,0:T(8,128)} %fusion.300) | copy-start | bytes 6148
  114.0 6.1 %copy-start.14 = (f32[16,32]{1,0:T(8,128)S(1)}, f32[16,32]{1,0:T(8,128)}, u32[]{:S(2)}) copy-start(f32[16,32]{1,0:T(8,128)} %fusion.295) | copy-start | bytes 6148
  120.0 4.0 %copy-start.15 = (f32[16,32]{1,0:T(8,128)S(1)}, f32[16,32]{1,0:T(8,128)}, u32[]{:S(2)}) copy-start(f32[16,32]{1,0:T(8,128)} %fusion.285) | copy-start | bytes 6148
  125.3 11.2 %copy-start.16 = (f32[2,256]{1,0:T(2,128)S(1)}, f32[2,256]{1,0:T(2,128)}, u32[]{:S(2)}) copy-start(f32[2,256]{1,0:T(2,128)} %fusion.250) | copy-start | bytes 6148
  127.4 11.3 %copy-start.5 = (bf16[2,256,64]{1,2,0:T(8,128)(2,1)S(1)}, bf16[2,256,64]{1,2,0:T(8,128)(2,1)}, u32[]{:S(2)}) copy-start(bf16[2,256,64]{1,2,0:T(8,128)(2,1)} %convolution_convert_fusion.9) | copy-start | bytes 196612
  127.4 11.4 %copy-start.6 = (bf16[2,256,64]{1,2,0:T(8,128)(2,1)S(1)}, bf16[2,256,64]{1,2,0:T(8,128)(2,1)}, u32[]{:S(2)}) copy-start(bf16[2,256,64]{1,2,0:T(8,128)(2,1)} %convolution_convert_fusion.10) | copy-start | bytes 196612
  129.6 27.4 %all-to-all-start.1 = ((bf16[32,16,512]{2,1,0:T(8,128)(2,1)}), bf16[32,16,512]{2,1,0:T(8,128)(2,1)}, u32[]{:S(2)}, u32[]{:S(2)}) async-start(bf16[32,16,512]{2,1,0:T(8,128)(2,1)} %copy.402), calls=%async_computation.1 | async-start | bytes 1048576 | tf_op jit(solution)/shard_map/all_to_all | solution.py:119
  155.4 7.0 %copy-start.12 = (f32[1024]{0:T(1024)S(1)}, f32[1024]{0:T(1024)}, u32[]{:S(2)}) copy-start(f32[1024]{0:T(1024)} %param.17) | copy-start | bytes 12292
where the time goes:
time: 168 us; the launch traced here: 166 us
  matrix products  105 us (62%)
  local copies, waits for them, and re-layouts  26.5 us (16%)
  starting transfers between devices  25.3 us (15%)
  waiting for transfers between devices  4.53 us (3%)
  other arithmetic  4.12 us (2%)
    dot_general x16, matrix products, attend_heads(): jnp.einsum(mixing_equation, attention_weights, value_operand, preferred_e...  31.9 us
    dot_general x16, matrix products, attend_heads(): jnp.einsum(scoring_equation, query_rows, key_operand, preferred_element_t...  30.3 us
    sub x16, matrix products, attend_heads(): attention_weights = jnp.exp(attention_logits - highest)  24.3 us
    dot_general x6, matrix products, project_three(): jnp.dot(flat_rows, qkv_weight[:, lower:upper], preferred_element_type=jnp...  15.1 us
    all_to_all x1, starting transfers between devices, on_device(): lax.all_to_all(normed, 'rows', split_axis=1, concat_axis=0, tiled=True)  14.6 us
    concatenate x9, local copies, waits for them, and re-layouts, on_device(): jnp.concatenate([row_heads, returned], axis=2).reshape(bands * width, model)  12.6 us
    all_to_all x1, starting transfers between devices, on_device(): lax.all_to_all(col_heads, 'rows', split_axis=0, concat_axis=1, tiled=True)  6.93 us
    ppermute x1, waiting for transfers between devices, with_halo(): after = lax.ppermute(leading, axis, down)  4.42 us
  transfers between devices with their start and end apart: 4, of which 2 were waited for; matrix products, arithmetic and copies ran while one was open for 26% of the time, Pallas kernels for 0%

commit v1 on v0

--- a/solution.py
+++ b/solution.py
@@ -116,7 +116,15 @@
     col_heads = attend_heads(
         col_query, col_key, col_value, col_count, tau_col, "lbd,mbd->blm", "blm,mbd->lbd"
     )
-    returned = lax.all_to_all(col_heads, "rows", split_axis=0, concat_axis=1, tiled=True)
+    ways, here = (lax.axis_size("rows"), lax.axis_index("rows"))
+    width_2 = col_heads.shape[0] // ways
+    turned = jnp.roll(col_heads, -here * width_2, axis=0)
+    got = [lax.slice_in_dim(turned, 0, width_2, axis=0)]
+    for far in range(1, ways):
+        sent = lax.slice_in_dim(turned, far * width_2, (far + 1) * width_2, axis=0)
+        got.append(lax.ppermute(sent, "rows", [(d, (d + far) % ways) for d in range(ways)]))
+    line = jnp.concatenate(got[::-1], axis=1)
+    returned = jnp.roll(line, (here + 1) * got[0].shape[1], axis=1)
     attended = jnp.concatenate([row_heads, returned], axis=2).reshape(bands * width, model)
     result = (
         mixed.reshape(bands * width, model).astype(jnp.float32)

time: 168 us -> 236 us (1.40)
  starting transfers between devices: 25.3 us -> 58.9 us
  waiting for transfers between devices: 4.53 us -> 24.3 us
  local copies, waits for them, and re-layouts: 26.5 us -> 37 us
  other arithmetic: 4.12 us -> 7.74 us
    ppermute x0 -> x15, starting transfers between devices: none -> 39.9 us  [on_device(): lax.ppermute(sent, 'rows', [(d, (d + far) % ways) for d in range(ways)])]
    ppermute x0 -> x15, waiting for transfers between devices: none -> 20.2 us  [on_device(): lax.ppermute(sent, 'rows', [(d, (d + far) % ways) for d in range(ways)])]
    convert_element_type x0 -> x8, local copies, waits for them, and re-layouts: none -> 9.25 us  [attend_heads(): outputs.append(jnp.einsum(mixing_equation, attention_weights, value_opera...]
    all_to_all x1 -> x0, starting transfers between devices: 6.93 us -> none  [on_device(): lax.all_to_all(col_heads, 'rows', split_axis=0, concat_axis=1, tiled=True)]
    unnamed x34 -> x69, local copies, waits for them, and re-layouts: 0.08 us -> 4.29 us
    concatenate x9 -> x2, local copies, waits for them, and re-layouts: 12.6 us -> 9.58 us  [on_device(): jnp.concatenate([row_heads, returned], axis=2).reshape(bands * width, model)]
  transfers between devices with their start and end apart: 4 -> 18, of which waited for: 2 -> 11; matrix products, arithmetic and copies ran while one was open for 26% -> 16% of each run, Pallas kernels for 0% -> 0%
where the time goes in v1:
time: 236 us; the launch traced here: 233 us
  matrix products  104 us (44%)
  starting transfers between devices  58.9 us (25%)
  local copies, waits for them, and re-layouts  37 us (16%)
  waiting for transfers between devices  24.3 us (10%)
  other arithmetic  7.74 us (3%)
    ppermute x15, starting transfers between devices, on_device(): lax.ppermute(sent, 'rows', [(d, (d + far) % ways) for d in range(ways)])  39.9 us
    dot_general x16, matrix products, attend_heads(): jnp.einsum(mixing_equation, attention_weights, value_operand, preferred_e...  32.1 us
    dot_general x16, matrix products, attend_heads(): jnp.einsum(scoring_equation, query_rows, key_operand, preferred_element_t...  30.4 us
    sub x16, matrix products, attend_heads(): attention_weights = jnp.exp(attention_logits - highest)  24.3 us
    ppermute x15, waiting for transfers between devices, on_device(): lax.ppermute(sent, 'rows', [(d, (d + far) % ways) for d in range(ways)])  20.2 us
    dot_general x6, matrix products, project_three(): jnp.dot(flat_rows, qkv_weight[:, lower:upper], preferred_element_type=jnp...  15.1 us
    all_to_all x1, starting transfers between devices, on_device(): lax.all_to_all(normed, 'rows', split_axis=1, concat_axis=0, tiled=True)  14.6 us
    concatenate x2, local copies, waits for them, and re-layouts, on_device(): jnp.concatenate([row_heads, returned], axis=2).reshape(bands * width, model)  9.58 us
  transfers between devices with their start and end apart: 18, of which 11 were waited for; matrix products, arithmetic and copies ran while one was open for 16% of the time, Pallas kernels for 0%

profile of v1, /device:TPU:0, one launch (start us, length us, event | category | flops | bytes accessed | tf_op | source)
XLA Modules:
  0.0 232.6 jit_solution(14194647368896380502)
XLA Ops:
  0.0 2.4 %fusion.240 = (bf16[1,256,1024]{2,1,0:T(8,128)(2,1)}, bf16[1,256,1024]{2,1,0:T(8,128)(2,1)}) fusion(bf16[2,256,1024]{2,1,0:T(8,128)(2,1)} %param.9), kind=kLoop, calls=%fused_computation.276 | loop fusion | bytes 2097152 | tf_op jit(solution)/shard_map/slice | solution.py:17
  2.4 3.2 %collective-permute-start = (bf16[1,256,1024]{2,1,0:T(8,128)(2,1)}, bf16[1,256,1024]{2,1,0:T(8,128)(2,1)}, u32[]{:S(2)}, u32[]{:S(2)}) collective-permute-start(bf16[1,256,1024]{2,1,0:T(8,128)(2,1)} %get-tuple-element.7), channel_id=1, source_target_pairs={{0,1},{1,2},{2,3},{3,4},{4,5},{5,6},{6,7},{7,8},{8,9},{9,10},{10,1... | collective-permute-start | bytes 1572872 | tf_op jit(solution)/shard_map/ppermute | solution.py:19
  7.0 4.0 %collective-permute-done.1 = bf16[1,256,1024]{2,1,0:T(8,128)(2,1)} collective-permute-done((bf16[1,256,1024]{2,1,0:T(8,128)(2,1)}, bf16[1,256,1024]{2,1,0:T(8,128)(2,1)}, u32[]{:S(2)}, u32[]{:S(2)}) %collective-permute-start.1) | collective-permute-done | bytes 524320 | tf_op jit(solution)/shard_map/ppermute | solution.py:20
  12.9 3.6 %convert_reduce_fusion = (f32[2,256]{1,0:T(2,128)S(1)}, bf16[2,256,1024]{2,1,0:T(8,128)(2,1)S(1)}) fusion(f32[1024]{0:T(1024)S(1)} %bitcast.118, bf16[4,258,1024]{2,1,0:T(8,128)(2,1)S(1)} %fusion.21, f32[1024]{0:T(1024)S(1)} %bitcast.119, bf16[1,256,1024]{2,1,0:T(8,128)(2,1)} %collective-permute-done.1, bf16[2,256,1024]{2,1,0:T(8,128)(2,1)S(1)} %copy-done.2, ...), kind=kLoop, calls=%fused_computation.41 | loop fusion | flops 17300992 | bytes 9480192 | tf_op jit(solution)/shard_map/reduce_sum | solution.py:38
  17.4 3.1 %fusion.35 = bf16[512,512]{1,0:T(8,128)(2,1)} fusion(bf16[512,1024]{1,0:T(8,128)(2,1)S(1)} %bitcast.68, bf16[1024,3072]{1,0:T(8,128)(2,1)} %param.14, f32[512]{0:T(512)S(1)} %get-tuple-element.60), kind=kOutput, calls=%fused_computation.49 | convolution fusion | flops 537395200 | bytes 2623488 | tf_op jit(solution)/shard_map/dot_general | solution.py:53
  20.6 2.8 %fusion.34 = bf16[512,512]{1,0:T(8,128)(2,1)} fusion(bf16[512,1024]{1,0:T(8,128)(2,1)S(1)} %bitcast.69, bf16[1024,3072]{1,0:T(8,128)(2,1)} %param.14, f32[512]{0:T(512)S(1)} %get-tuple-element.61), kind=kOutput, calls=%fused_computation.48 | convolution fusion | flops 537395200 | bytes 2623488 | tf_op jit(solution)/shard_map/dot_general | solution.py:53
  43.2 2.8 %fusion.36 = bf16[512,512]{1,0:T(8,128)(2,1)} fusion(bf16[512,1024]{1,0:T(8,128)(2,1)S(1)} %bitcast.70, bf16[1024,3072]{1,0:T(8,128)(2,1)} %param.14, f32[512]{0:T(512)S(1)} %get-tuple-element.59), kind=kOutput, calls=%fused_computation.50 | convolution fusion | flops 537395200 | bytes 2623488 | tf_op jit(solution)/shard_map/dot_general | solution.py:53
  46.0 14.6 %all-to-all-start = ((bf16[2,256,1024]{2,0,1:T(2,128)(2,1)}), bf16[2,256,1024]{2,0,1:T(2,128)(2,1)}, u32[]{:S(2)}, u32[]{:S(2)}) async-start(bf16[2,256,1024]{2,0,1:T(2,128)(2,1)} %copy.343), calls=%async_computation | async-start | bytes 2097152 | tf_op jit(solution)/shard_map/all_to_all | solution.py:107
  77.3 2.2 convolution_convert_fusion.14
  87.5 2.3 fusion.39
  120.0 2.2 fusion.37
  143.5 4.4 %collective-permute-start.2 = (bf16[2,16,512]{2,0,1:T(2,128)(2,1)}, bf16[2,16,512]{2,0,1:T(2,128)(2,1)}, u32[]{:S(2)}, u32[]{:S(2)}) collective-permute-start(bf16[2,16,512]{2,0,1:T(2,128)(2,1)} %get-tuple-element.23), channel_id=1, source_target_pairs={{0,15},{1,0},{2,1},{3,2},{4,3},{5,4},{6,5},{7,6},{8,7},{9,8},{10,9... | collective-permute-start | bytes 98312 | tf_op jit(solution)/shard_map/ppermute | solution.py:125
  161.1 4.2 %collective-permute-start.3 = (bf16[2,16,512]{2,0,1:T(2,128)(2,1)}, bf16[2,16,512]{2,0,1:T(2,128)(2,1)S(1)}, u32[]{:S(2)}, u32[]{:S(2)}) collective-permute-start(bf16[2,16,512]{2,0,1:T(2,128)(2,1)} %get-tuple-element.22), channel_id=1, source_target_pairs={{0,14},{1,15},{2,0},{3,1},{4,2},{5,3},{6,4},{7,5},{8,6},{9,7},{10,... | collective-permute-start | bytes 98312 | tf_op jit(solution)/shard_map/ppermute | solution.py:125
  167.2 3.5 %collective-permute-done.4 = bf16[2,16,512]{2,0,1:T(2,128)(2,1)S(1)} collective-permute-done((bf16[2,16,512]{2,0,1:T(2,128)(2,1)}, bf16[2,16,512]{2,0,1:T(2,128)(2,1)S(1)}, u32[]{:S(2)}, u32[]{:S(2)}) %collective-permute-start.4) | collective-permute-done | bytes 32800 | tf_op jit(solution)/shard_map/ppermute | solution.py:125
  172.6 2.2 collective-permute-done.5
  174.8 2.6 %collective-permute-start.6 = (bf16[2,16,512]{2,0,1:T(2,128)(2,1)}, bf16[2,16,512]{2,0,1:T(2,128)(2,1)S(1)}, u32[]{:S(2)}, u32[]{:S(2)}) collective-permute-start(bf16[2,16,512]{2,0,1:T(2,128)(2,1)} %get-tuple-element.19), channel_id=1, source_target_pairs={{0,11},{1,12},{2,13},{3,14},{4,15},{5,0},{6,1},{7,2},{8,3},{9,4},{... | collective-permute-start | bytes 98312 | tf_op jit(solution)/shard_map/ppermute | solution.py:125
  179.3 5.2 %collective-permute-start.7 = (bf16[2,16,512]{2,0,1:T(2,128)(2,1)}, bf16[2,16,512]{2,0,1:T(2,128)(2,1)S(1)}, u32[]{:S(2)}, u32[]{:S(2)}) collective-permute-start(bf16[2,16,512]{2,0,1:T(2,128)(2,1)} %get-tuple-element.18), channel_id=1, source_target_pairs={{0,10},{1,11},{2,12},{3,13},{4,14},{5,15},{6,0},{7,1},{8,2},{9,3},... | collective-permute-start | bytes 98312 | tf_op jit(solution)/shard_map/ppermute | solution.py:125
  186.4 3.8 %collective-permute-start.8 = (bf16[2,16,512]{2,0,1:T(2,128)(2,1)}, bf16[2,16,512]{2,0,1:T(2,128)(2,1)S(1)}, u32[]{:S(2)}, u32[]{:S(2)}) collective-permute-start(bf16[2,16,512]{2,0,1:T(2,128)(2,1)} %get-tuple-element.17), channel_id=1, source_target_pairs={{0,9},{1,10},{2,11},{3,12},{4,13},{5,14},{6,15},{7,0},{8,1},{9,2},... | collective-permute-start | bytes 98312 | tf_op jit(solution)/shard_map/ppermute | solution.py:125
  192.1 4.6 %collective-permute-start.9 = (bf16[2,16,512]{2,0,1:T(2,128)(2,1)}, bf16[2,16,512]{2,0,1:T(2,128)(2,1)S(1)}, u32[]{:S(2)}, u32[]{:S(2)}) collective-permute-start(bf16[2,16,512]{2,0,1:T(2,128)(2,1)} %get-tuple-element.16), channel_id=1, source_target_pairs={{0,8},{1,9},{2,10},{3,11},{4,12},{5,13},{6,14},{7,15},{8,0},{9,1},... | collective-permute-start | bytes 98312 | tf_op jit(solution)/shard_map/ppermute | solution.py:125
  198.8 2.7 %collective-permute-start.10 = (bf16[2,16,512]{2,0,1:T(2,128)(2,1)}, bf16[2,16,512]{2,0,1:T(2,128)(2,1)S(1)}, u32[]{:S(2)}, u32[]{:S(2)}) collective-permute-start(bf16[2,16,512]{2,0,1:T(2,128)(2,1)} %get-tuple-element.15), channel_id=1, source_target_pairs={{0,7},{1,8},{2,9},{3,10},{4,11},{5,12},{6,13},{7,14},{8,15},{9,0},... | collective-permute-start | bytes 98312 | tf_op jit(solution)/shard_map/ppermute | solution.py:125
  203.4 5.2 %collective-permute-start.11 = (bf16[2,16,512]{2,0,1:T(2,128)(2,1)}, bf16[2,16,512]{2,0,1:T(2,128)(2,1)S(1)}, u32[]{:S(2)}, u32[]{:S(2)}) collective-permute-start(bf16[2,16,512]{2,0,1:T(2,128)(2,1)} %get-tuple-element.14), channel_id=1, source_target_pairs={{0,6},{1,7},{2,8},{3,9},{4,10},{5,11},{6,12},{7,13},{8,14},{9,15},... | collective-permute-start | bytes 98312 | tf_op jit(solution)/shard_map/ppermute | solution.py:125
  210.5 3.8 %collective-permute-start.12 = (bf16[2,16,512]{2,0,1:T(2,128)(2,1)}, bf16[2,16,512]{2,0,1:T(2,128)(2,1)S(1)}, u32[]{:S(2)}, u32[]{:S(2)}) collective-permute-start(bf16[2,16,512]{2,0,1:T(2,128)(2,1)} %get-tuple-element.13), channel_id=1, source_target_pairs={{0,5},{1,6},{2,7},{3,8},{4,9},{5,10},{6,11},{7,12},{8,13},{9,14},{... | collective-permute-start | bytes 98312 | tf_op jit(solution)/shard_map/ppermute | solution.py:125
  220.8 8.1 %concatenate.31 = bf16[2,256,1024]{2,0,1:T(2,128)(2,1)} concatenate(bf16[2,256,64]{2,0,1:T(2,128)(2,1)} %copy.378, bf16[2,256,64]{2,0,1:T(2,128)(2,1)} %copy.379, bf16[2,256,64]{2,0,1:T(2,128)(2,1)} %copy.380, bf16[2,256,64]{2,0,1:T(2,128)(2,1)} %copy.381, bf16[2,256,64]{2,0,1:T(2,128)(2,1)S(1)} %copy.382, bf16[2,256,64]{2,0,1:T(2,128)(2,1)S(1)} %copy.383, ...), dimensions={2} | concatenate | bytes 2097152 | tf_op jit(solution)/shard_map/concatenate | solution.py:128
  230.4 2.2 fusion.33
  (165 shorter events, 136.5 us)
Async XLA Ops:
  0.0 230.4 %copy-start = (bf16[1024,1024]{1,0:T(8,128)(2,1)S(1)}, bf16[1024,1024]{1,0:T(8,128)(2,1)}, u32[]{:S(2)}) copy-start(bf16[1024,1024]{1,0:T(8,128)(2,1)} %param.16) | copy-start | bytes 6291460
  0.0 11.0 %copy-start.1 = (bf16[2,256,1024]{2,1,0:T(8,128)(2,1)S(1)}, bf16[2,256,1024]{2,1,0:T(8,128)(2,1)}, u32[]{:S(2)}) copy-start(bf16[2,256,1024]{2,1,0:T(8,128)(2,1)} %param.9) | copy-start | bytes 3145732
  2.4 4.6 %collective-permute-start = (bf16[1,256,1024]{2,1,0:T(8,128)(2,1)}, bf16[1,256,1024]{2,1,0:T(8,128)(2,1)}, u32[]{:S(2)}, u32[]{:S(2)}) collective-permute-start(bf16[1,256,1024]{2,1,0:T(8,128)(2,1)} %get-tuple-element.7), channel_id=1, source_target_pairs={{0,1},{1,2},{2,3},{3,4},{4,5},{5,6},{6,7},{7,8},{8,9},{9,10},{10,1... | collective-permute-start | bytes 1572872 | tf_op jit(solution)/shard_map/ppermute | solution.py:19
  5.6 5.5 %collective-permute-start.1 = (bf16[1,256,1024]{2,1,0:T(8,128)(2,1)}, bf16[1,256,1024]{2,1,0:T(8,128)(2,1)}, u32[]{:S(2)}, u32[]{:S(2)}) collective-permute-start(bf16[1,256,1024]{2,1,0:T(8,128)(2,1)} %get-tuple-element.8), channel_id=1, source_target_pairs={{1,0},{2,1},{3,2},{4,3},{5,4},{6,5},{7,6},{8,7},{9,8},{10,9},{11,1... | collective-permute-start | bytes 1572872 | tf_op jit(solution)/shard_map/ppermute | solution.py:20
  46.0 39.9 %all-to-all-start = ((bf16[2,256,1024]{2,0,1:T(2,128)(2,1)}), bf16[2,256,1024]{2,0,1:T(2,128)(2,1)}, u32[]{:S(2)}, u32[]{:S(2)}) async-start(bf16[2,256,1024]{2,0,1:T(2,128)(2,1)} %copy.343), calls=%async_computation | async-start | bytes 2097152 | tf_op jit(solution)/shard_map/all_to_all | solution.py:107
  138.0 9.9 %copy-start.18 = (f32[2,256]{1,0:T(2,128)S(1)}, f32[2,256]{1,0:T(2,128)}, u32[]{:S(2)}) copy-start(f32[2,256]{1,0:T(2,128)} %fusion.247) | copy-start | bytes 6148
  140.2 10.0 %copy-start.7 = (bf16[2,256,64]{1,2,0:T(8,128)(2,1)S(1)}, bf16[2,256,64]{1,2,0:T(8,128)(2,1)}, u32[]{:S(2)}) copy-start(bf16[2,256,64]{1,2,0:T(8,128)(2,1)} %convolution_convert_fusion.9) | copy-start | bytes 196612
  140.2 10.1 %copy-start.8 = (bf16[2,256,64]{1,2,0:T(8,128)(2,1)S(1)}, bf16[2,256,64]{1,2,0:T(8,128)(2,1)}, u32[]{:S(2)}) copy-start(bf16[2,256,64]{1,2,0:T(8,128)(2,1)} %convolution_convert_fusion.10) | copy-start | bytes 196612
  143.5 17.5 %collective-permute-start.2 = (bf16[2,16,512]{2,0,1:T(2,128)(2,1)}, bf16[2,16,512]{2,0,1:T(2,128)(2,1)}, u32[]{:S(2)}, u32[]{:S(2)}) collective-permute-start(bf16[2,16,512]{2,0,1:T(2,128)(2,1)} %get-tuple-element.23), channel_id=1, source_target_pairs={{0,15},{1,0},{2,1},{3,2},{4,3},{5,4},{6,5},{7,6},{8,7},{9,8},{10,9... | collective-permute-start | bytes 98312 | tf_op jit(solution)/shard_map/ppermute | solution.py:125
  159.4 57.0 %collective-permute-start.16 = (bf16[2,16,512]{2,0,1:T(2,128)(2,1)}, bf16[2,16,512]{2,0,1:T(2,128)(2,1)S(1)}, u32[]{:S(2)}, u32[]{:S(2)}) collective-permute-start(bf16[2,16,512]{2,0,1:T(2,128)(2,1)} %get-tuple-element.9), channel_id=1, source_target_pairs={{0,1},{1,2},{2,3},{3,4},{4,5},{5,6},{6,7},{7,8},{8,9},{9,10},{10,1... | collective-permute-start | bytes 98312 | tf_op jit(solution)/shard_map/ppermute | solution.py:125
  159.4 56.9 %collective-permute-start.15 = (bf16[2,16,512]{2,0,1:T(2,128)(2,1)}, bf16[2,16,512]{2,0,1:T(2,128)(2,1)S(1)}, u32[]{:S(2)}, u32[]{:S(2)}) collective-permute-start(bf16[2,16,512]{2,0,1:T(2,128)(2,1)} %get-tuple-element.10), channel_id=1, source_target_pairs={{0,2},{1,3},{2,4},{3,5},{4,6},{5,7},{6,8},{7,9},{8,10},{9,11},{10,... | collective-permute-start | bytes 98312 | tf_op jit(solution)/shard_map/ppermute | solution.py:125
  159.4 56.9 %collective-permute-start.14 = (bf16[2,16,512]{2,0,1:T(2,128)(2,1)}, bf16[2,16,512]{2,0,1:T(2,128)(2,1)S(1)}, u32[]{:S(2)}, u32[]{:S(2)}) collective-permute-start(bf16[2,16,512]{2,0,1:T(2,128)(2,1)} %get-tuple-element.11), channel_id=1, source_target_pairs={{0,3},{1,4},{2,5},{3,6},{4,7},{5,8},{6,9},{7,10},{8,11},{9,12},{10... | collective-permute-start | bytes 98312 | tf_op jit(solution)/shard_map/ppermute | solution.py:125
  159.6 56.6 %collective-permute-start.13 = (bf16[2,16,512]{2,0,1:T(2,128)(2,1)}, bf16[2,16,512]{2,0,1:T(2,128)(2,1)S(1)}, u32[]{:S(2)}, u32[]{:S(2)}) collective-permute-start(bf16[2,16,512]{2,0,1:T(2,128)(2,1)} %get-tuple-element.12), channel_id=1, source_target_pairs={{0,4},{1,5},{2,6},{3,7},{4,8},{5,9},{6,10},{7,11},{8,12},{9,13},{1... | collective-permute-start | bytes 98312 | tf_op jit(solution)/shard_map/ppermute | solution.py:125
  161.1 6.1 %collective-permute-start.3 = (bf16[2,16,512]{2,0,1:T(2,128)(2,1)}, bf16[2,16,512]{2,0,1:T(2,128)(2,1)S(1)}, u32[]{:S(2)}, u32[]{:S(2)}) collective-permute-start(bf16[2,16,512]{2,0,1:T(2,128)(2,1)} %get-tuple-element.22), channel_id=1, source_target_pairs={{0,14},{1,15},{2,0},{3,1},{4,2},{5,3},{6,4},{7,5},{8,6},{9,7},{10,... | collective-permute-start | bytes 98312 | tf_op jit(solution)/shard_map/ppermute | solution.py:125
  167.1 3.6 %collective-permute-start.4 = (bf16[2,16,512]{2,0,1:T(2,128)(2,1)}, bf16[2,16,512]{2,0,1:T(2,128)(2,1)S(1)}, u32[]{:S(2)}, u32[]{:S(2)}) collective-permute-start(bf16[2,16,512]{2,0,1:T(2,128)(2,1)} %get-tuple-element.21), channel_id=1, source_target_pairs={{0,13},{1,14},{2,15},{3,0},{4,1},{5,2},{6,3},{7,4},{8,5},{9,6},{10... | collective-permute-start | bytes 98312 | tf_op jit(solution)/shard_map/ppermute | solution.py:125
  170.7 4.1 %collective-permute-start.5 = (bf16[2,16,512]{2,0,1:T(2,128)(2,1)}, bf16[2,16,512]{2,0,1:T(2,128)(2,1)S(1)}, u32[]{:S(2)}, u32[]{:S(2)}) collective-permute-start(bf16[2,16,512]{2,0,1:T(2,128)(2,1)} %get-tuple-element.20), channel_id=1, source_target_pairs={{0,12},{1,13},{2,14},{3,15},{4,0},{5,1},{6,2},{7,3},{8,4},{9,5},{1... | collective-permute-start | bytes 98312 | tf_op jit(solution)/shard_map/ppermute | solution.py:125
  174.8 4.5 %collective-permute-start.6 = (bf16[2,16,512]{2,0,1:T(2,128)(2,1)}, bf16[2,16,512]{2,0,1:T(2,128)(2,1)S(1)}, u32[]{:S(2)}, u32[]{:S(2)}) collective-permute-start(bf16[2,16,512]{2,0,1:T(2,128)(2,1)} %get-tuple-element.19), channel_id=1, source_target_pairs={{0,11},{1,12},{2,13},{3,14},{4,15},{5,0},{6,1},{7,2},{8,3},{9,4},{... | collective-permute-start | bytes 98312 | tf_op jit(solution)/shard_map/ppermute | solution.py:125
  179.3 7.1 %collective-permute-start.7 = (bf16[2,16,512]{2,0,1:T(2,128)(2,1)}, bf16[2,16,512]{2,0,1:T(2,128)(2,1)S(1)}, u32[]{:S(2)}, u32[]{:S(2)}) collective-permute-start(bf16[2,16,512]{2,0,1:T(2,128)(2,1)} %get-tuple-element.18), channel_id=1, source_target_pairs={{0,10},{1,11},{2,12},{3,13},{4,14},{5,15},{6,0},{7,1},{8,2},{9,3},... | collective-permute-start | bytes 98312 | tf_op jit(solution)/shard_map/ppermute | solution.py:125
  186.4 5.7 %collective-permute-start.8 = (bf16[2,16,512]{2,0,1:T(2,128)(2,1)}, bf16[2,16,512]{2,0,1:T(2,128)(2,1)S(1)}, u32[]{:S(2)}, u32[]{:S(2)}) collective-permute-start(bf16[2,16,512]{2,0,1:T(2,128)(2,1)} %get-tuple-element.17), channel_id=1, source_target_pairs={{0,9},{1,10},{2,11},{3,12},{4,13},{5,14},{6,15},{7,0},{8,1},{9,2},... | collective-permute-start | bytes 98312 | tf_op jit(solution)/shard_map/ppermute | solution.py:125
  192.1 6.7 %collective-permute-start.9 = (bf16[2,16,512]{2,0,1:T(2,128)(2,1)}, bf16[2,16,512]{2,0,1:T(2,128)(2,1)S(1)}, u32[]{:S(2)}, u32[]{:S(2)}) collective-permute-start(bf16[2,16,512]{2,0,1:T(2,128)(2,1)} %get-tuple-element.16), channel_id=1, source_target_pairs={{0,8},{1,9},{2,10},{3,11},{4,12},{5,13},{6,14},{7,15},{8,0},{9,1},... | collective-permute-start | bytes 98312 | tf_op jit(solution)/shard_map/ppermute | solution.py:125
  198.8 4.6 %collective-permute-start.10 = (bf16[2,16,512]{2,0,1:T(2,128)(2,1)}, bf16[2,16,512]{2,0,1:T(2,128)(2,1)S(1)}, u32[]{:S(2)}, u32[]{:S(2)}) collective-permute-start(bf16[2,16,512]{2,0,1:T(2,128)(2,1)} %get-tuple-element.15), channel_id=1, source_target_pairs={{0,7},{1,8},{2,9},{3,10},{4,11},{5,12},{6,13},{7,14},{8,15},{9,0},... | collective-permute-start | bytes 98312 | tf_op jit(solution)/shard_map/ppermute | solution.py:125
  203.4 7.1 %collective-permute-start.11 = (bf16[2,16,512]{2,0,1:T(2,128)(2,1)}, bf16[2,16,512]{2,0,1:T(2,128)(2,1)S(1)}, u32[]{:S(2)}, u32[]{:S(2)}) collective-permute-start(bf16[2,16,512]{2,0,1:T(2,128)(2,1)} %get-tuple-element.14), channel_id=1, source_target_pairs={{0,6},{1,7},{2,8},{3,9},{4,10},{5,11},{6,12},{7,13},{8,14},{9,15},... | collective-permute-start | bytes 98312 | tf_op jit(solution)/shard_map/ppermute | solution.py:125
  210.5 5.7 %collective-permute-start.12 = (bf16[2,16,512]{2,0,1:T(2,128)(2,1)}, bf16[2,16,512]{2,0,1:T(2,128)(2,1)S(1)}, u32[]{:S(2)}, u32[]{:S(2)}) collective-permute-start(bf16[2,16,512]{2,0,1:T(2,128)(2,1)} %get-tuple-element.13), channel_id=1, source_target_pairs={{0,5},{1,6},{2,7},{3,8},{4,9},{5,10},{6,11},{7,12},{8,13},{9,14},{... | collective-permute-start | bytes 98312 | tf_op jit(solution)/shard_map/ppermute | solution.py:125
  220.8 9.6 %copy-start.14 = (f32[1024]{0:T(1024)S(1)}, f32[1024]{0:T(1024)}, u32[]{:S(2)}) copy-start(f32[1024]{0:T(1024)} %param.17) | copy-start | bytes 12292
  (13 other events, 69.1 us)
